TPU v7x, 256 devices: a whole 4x4x8 slice. The times are simulated.
256 devices in a mesh: grp: 8 (over x, core), lx: 4 (over y), ly: 8 (over z).
Axes of the slice: x: 4, y: 4, z: 8, core: 2. Of those that a mesh axis runs over, the one named last changes fastest.
Arguments:
- vectors: float32 [32, 256, 4096], P('grp', 'lx', 'ly'), may hold values from -6 to 6
- levels: int32 [256, 4096], P('lx', 'ly'), may hold values from 0 to 7
- level_table: float32 [8], replicated, may hold values from 1 to 3
- filter_low: float32 [1], replicated, may hold values from -1 to 0.5
- filter_high: float32 [1], replicated, may hold values from 6 to 7.5
Outputs:
- basis: float32 [32, 256, 4096], P('grp', 'lx', 'ly')
All inputs are finite; a program needn't handle non-finite values.
Results may differ from a plain program's by a relative error of at most 0.00011.
Values sent between devices are 32-bit elements; how exact they have to be, the bound alone decides.
No kernel may reach another device: no remote copies, remote signals or barrier semaphores. Data moves between devices by JAX's collectives and lax.ppermute only.
A program may use at most 64 MiB of HBM per device.

v0:
```python
import jax
import jax.numpy as jnp
from jax import lax
from jax.sharding import PartitionSpec as P


def padded_2(shard, sides, width):
    for axis, dim in sides:
        size, length = (lax.axis_size(axis), shard.shape[dim])
        up = [(i, (i + 1) % size) for i in range(size)]
        down = [(j, i) for i, j in up]
        last = lax.slice_in_dim(shard, length - width, length, axis=dim)
        leading = lax.slice_in_dim(shard, 0, width, axis=dim)
        before = lax.ppermute(last, axis, up)
        after = lax.ppermute(leading, axis, down)
        shard = jnp.concatenate([before, shard, after], axis=dim)
    return shard


def from_root(value, axis, source):
    kept = jnp.where(lax.axis_index(axis) == source, value, 0).astype(value.dtype)
    return lax.psum(kept, axis)


def apply_operator(field, onsite):
    padded = padded_2(field, (("lx", 1), ("ly", 2)), 1)
    beside = padded[:, 2:, 1:-1] + padded[:, :-2, 1:-1] + padded[:, 1:-1, 2:] + padded[:, 1:-1, :-2]
    return onsite[None] * field - beside


def lower_inverse(gram):
    lower = jnp.linalg.cholesky(gram)
    eye_block = jnp.eye(gram.shape[0], dtype=jnp.float32)
    return lax.linalg.triangular_solve(lower, eye_block, left_side=True, lower=True)


def body(vectors, levels, level_table, filter_low, filter_high):
    count_vec, rows_local, cols_local = vectors.shape
    level_ids = jnp.arange(level_table.shape[0], dtype=jnp.int32)
    onsite = jnp.sum(
        jnp.where(levels[None] == level_ids[:, None, None], level_table[:, None, None], 0.0), axis=0
    )
    center = (filter_high[0] + filter_low[0]) / 2.0
    half = (filter_high[0] - filter_low[0]) / 2.0
    first = (apply_operator(vectors, onsite) - center * vectors) / half
    filtered = 2.0 * (apply_operator(first, onsite) - center * first) / half - vectors
    total = rows_local * cols_local * lax.axis_size("lx") * lax.axis_size("ly")
    flat = filtered.reshape(count_vec, rows_local * cols_local)
    highest = lax.Precision.HIGHEST
    mine = lax.axis_index("grp")
    result = jnp.zeros_like(flat)
    for h in range(lax.axis_size("grp")):
        gram = lax.psum(jnp.dot(flat, flat.T, precision=highest), ("lx", "ly")) / total
        done = jnp.dot(lower_inverse(gram), flat, precision=highest)
        result = jnp.where(mine == h, done, result)
        shared = from_root(done, "grp", h)
        coeff = lax.psum(jnp.dot(shared, flat.T, precision=highest), ("lx", "ly")) / total
        later = mine > h
        flat = jnp.where(later, flat - jnp.dot(coeff.T, shared, precision=highest), flat)
    return result.reshape(count_vec, rows_local, cols_local)


def solution(mesh):
    in_specs = (P("grp", "lx", "ly"), P("lx", "ly"), P(), P(), P())
    out_specs = P("grp", "lx", "ly")
    return jax.shard_map(body, mesh=mesh, in_specs=in_specs, out_specs=out_specs, check_vma=False)
```

profile of v0, /device:TPU:32, one launch (start us, length us, event | category | flops | bytes accessed | tf_op | source)
XLA Modules:
  0.0 1632.8 jit_solution(7607256732290742390)
XLA Ops:
  11.9 3.5 collective-permute-done.1
  21.7 3.9 collective-permute-done.3
  31.3 3.3 collective-permute-start.6
  42.6 71.0 %psum.154 = f32[4,4]{0,1:T(4,128)S(1)} all-reduce(f32[4,4]{0,1:T(4,128)S(1)} %convolution_bitcast_fusion), channel_id=1, replica_groups=mesh['grp'=8,'lx'=4,'ly'=8] {'lx','ly'}, use_global_device_ids=true, to_apply=%region_1.2 | all-reduce | flops 16 | bytes 128 | tf_op jit(solution)/shard_map/psum | solution.py:53
  118.3 60.3 %all-reduce.8.cloned.1.call-done = f32[4,32768]{1,0:T(4,128)} async-done(((f32[4,32768]{1,0:T(4,128)}), f32[4,32768]{1,0:T(4,128)}) %all-reduce.8.cloned.1.call-update) | async-done | bytes 524304 | tf_op jit(solution)/shard_map/psum | solution.py:22
  178.6 3.5 fusion.99
  182.1 71.6 %psum.156 = f32[4,4]{0,1:T(4,128)S(1)} all-reduce(f32[4,4]{0,1:T(4,128)S(1)} %fusion.99), channel_id=1, replica_groups=mesh['grp'=8,'lx'=4,'ly'=8] {'lx','ly'}, use_global_device_ids=true, to_apply=%region_5.8 | all-reduce | flops 16 | bytes 128 | tf_op jit(solution)/shard_map/psum | solution.py:57
  257.1 73.6 %psum.157 = f32[4,4]{0,1:T(4,128)S(1)} all-reduce(f32[4,4]{0,1:T(4,128)S(1)} %fusion.100), channel_id=1, replica_groups=mesh['grp'=8,'lx'=4,'ly'=8] {'lx','ly'}, use_global_device_ids=true, to_apply=%region_6.9 | all-reduce | flops 16 | bytes 128 | tf_op jit(solution)/shard_map/psum | solution.py:53
  335.0 58.1 %all-reduce.10.cloned.1.call-done = f32[4,32768]{1,0:T(4,128)} async-done(((f32[4,32768]{1,0:T(4,128)}), f32[4,32768]{1,0:T(4,128)}) %all-reduce.10.cloned.1.call-update) | async-done | bytes 524304 | tf_op jit(solution)/shard_map/psum | solution.py:22
  393.1 3.5 fusion.101
  396.6 71.6 %psum.159 = f32[4,4]{0,1:T(4,128)S(1)} all-reduce(f32[4,4]{0,1:T(4,128)S(1)} %fusion.101), channel_id=1, replica_groups=mesh['grp'=8,'lx'=4,'ly'=8] {'lx','ly'}, use_global_device_ids=true, to_apply=%region_8.11 | all-reduce | flops 16 | bytes 128 | tf_op jit(solution)/shard_map/psum | solution.py:57
  471.6 73.6 %psum.160 = f32[4,4]{0,1:T(4,128)S(1)} all-reduce(f32[4,4]{0,1:T(4,128)S(1)} %fusion.102), channel_id=1, replica_groups=mesh['grp'=8,'lx'=4,'ly'=8] {'lx','ly'}, use_global_device_ids=true, to_apply=%region_9.12 | all-reduce | flops 16 | bytes 128 | tf_op jit(solution)/shard_map/psum | solution.py:53
  549.8 57.8 %all-reduce.12.cloned.1.call-done = f32[4,32768]{1,0:T(4,128)} async-done(((f32[4,32768]{1,0:T(4,128)}), f32[4,32768]{1,0:T(4,128)}) %all-reduce.12.cloned.1.call-update) | async-done | bytes 524304 | tf_op jit(solution)/shard_map/psum | solution.py:22
  607.6 3.5 fusion.103
  611.1 71.6 %psum.162 = f32[4,4]{0,1:T(4,128)S(1)} all-reduce(f32[4,4]{0,1:T(4,128)S(1)} %fusion.103), channel_id=1, replica_groups=mesh['grp'=8,'lx'=4,'ly'=8] {'lx','ly'}, use_global_device_ids=true, to_apply=%region_11.14 | all-reduce | flops 16 | bytes 128 | tf_op jit(solution)/shard_map/psum | solution.py:57
  686.1 73.6 %psum.163 = f32[4,4]{0,1:T(4,128)S(1)} all-reduce(f32[4,4]{0,1:T(4,128)S(1)} %fusion.104), channel_id=1, replica_groups=mesh['grp'=8,'lx'=4,'ly'=8] {'lx','ly'}, use_global_device_ids=true, to_apply=%region_12.15 | all-reduce | flops 16 | bytes 128 | tf_op jit(solution)/shard_map/psum | solution.py:53
  764.0 58.1 %all-reduce.14.cloned.1.call-done = f32[4,32768]{1,0:T(4,128)} async-done(((f32[4,32768]{1,0:T(4,128)}), f32[4,32768]{1,0:T(4,128)}) %all-reduce.14.cloned.1.call-update) | async-done | bytes 524304 | tf_op jit(solution)/shard_map/psum | solution.py:22
  822.1 3.5 fusion.105
  825.6 71.6 %psum.165 = f32[4,4]{0,1:T(4,128)S(1)} all-reduce(f32[4,4]{0,1:T(4,128)S(1)} %fusion.105), channel_id=1, replica_groups=mesh['grp'=8,'lx'=4,'ly'=8] {'lx','ly'}, use_global_device_ids=true, to_apply=%region_14.17 | all-reduce | flops 16 | bytes 128 | tf_op jit(solution)/shard_map/psum | solution.py:57
  900.6 73.6 %psum.166 = f32[4,4]{0,1:T(4,128)S(1)} all-reduce(f32[4,4]{0,1:T(4,128)S(1)} %fusion.106), channel_id=1, replica_groups=mesh['grp'=8,'lx'=4,'ly'=8] {'lx','ly'}, use_global_device_ids=true, to_apply=%region_15.18 | all-reduce | flops 16 | bytes 128 | tf_op jit(solution)/shard_map/psum | solution.py:53
  978.9 57.6 %all-reduce.16.cloned.1.call-done = f32[4,32768]{1,0:T(4,128)} async-done(((f32[4,32768]{1,0:T(4,128)}), f32[4,32768]{1,0:T(4,128)}) %all-reduce.16.cloned.1.call-update) | async-done | bytes 524304 | tf_op jit(solution)/shard_map/psum | solution.py:22
  1036.6 3.5 fusion.107
  1040.0 71.6 %psum.168 = f32[4,4]{0,1:T(4,128)S(1)} all-reduce(f32[4,4]{0,1:T(4,128)S(1)} %fusion.107), channel_id=1, replica_groups=mesh['grp'=8,'lx'=4,'ly'=8] {'lx','ly'}, use_global_device_ids=true, to_apply=%region_17.20 | all-reduce | flops 16 | bytes 128 | tf_op jit(solution)/shard_map/psum | solution.py:57
  1116.0 73.6 %psum.169 = f32[4,4]{0,1:T(4,128)S(1)} all-reduce(f32[4,4]{0,1:T(4,128)S(1)} %fusion.108), channel_id=1, replica_groups=mesh['grp'=8,'lx'=4,'ly'=8] {'lx','ly'}, use_global_device_ids=true, to_apply=%region_18.21 | all-reduce | flops 16 | bytes 128 | tf_op jit(solution)/shard_map/psum | solution.py:53
  1194.2 58.1 %all-reduce.18.cloned.1.call-done = f32[4,32768]{1,0:T(4,128)} async-done(((f32[4,32768]{1,0:T(4,128)}), f32[4,32768]{1,0:T(4,128)}) %all-reduce.18.cloned.1.call-update) | async-done | bytes 524304 | tf_op jit(solution)/shard_map/psum | solution.py:22
  1252.2 3.5 fusion.109
  1255.7 71.6 %psum.171 = f32[4,4]{0,1:T(4,128)S(1)} all-reduce(f32[4,4]{0,1:T(4,128)S(1)} %fusion.109), channel_id=1, replica_groups=mesh['grp'=8,'lx'=4,'ly'=8] {'lx','ly'}, use_global_device_ids=true, to_apply=%region_20.23 | all-reduce | flops 16 | bytes 128 | tf_op jit(solution)/shard_map/psum | solution.py:57
  1331.6 73.8 %psum.172 = f32[4,4]{0,1:T(4,128)S(1)} all-reduce(f32[4,4]{0,1:T(4,128)S(1)} %fusion.110), channel_id=1, replica_groups=mesh['grp'=8,'lx'=4,'ly'=8] {'lx','ly'}, use_global_device_ids=true, to_apply=%region_21.24 | all-reduce | flops 16 | bytes 128 | tf_op jit(solution)/shard_map/psum | solution.py:53
  1409.9 58.1 %all-reduce.20.cloned.1.call-done = f32[4,32768]{1,0:T(4,128)} async-done(((f32[4,32768]{1,0:T(4,128)}), f32[4,32768]{1,0:T(4,128)}) %all-reduce.20.cloned.1.call-update) | async-done | bytes 524304 | tf_op jit(solution)/shard_map/psum | solution.py:22
  1468.0 3.5 fusion.111
  1471.5 71.6 %psum.174 = f32[4,4]{0,1:T(4,128)S(1)} all-reduce(f32[4,4]{0,1:T(4,128)S(1)} %fusion.111), channel_id=1, replica_groups=mesh['grp'=8,'lx'=4,'ly'=8] {'lx','ly'}, use_global_device_ids=true, to_apply=%region_23.26 | all-reduce | flops 16 | bytes 128 | tf_op jit(solution)/shard_map/psum | solution.py:57
  1547.5 73.6 %psum.175 = f32[4,4]{0,1:T(4,128)S(1)} all-reduce(f32[4,4]{0,1:T(4,128)S(1)} %fusion.112), channel_id=1, replica_groups=mesh['grp'=8,'lx'=4,'ly'=8] {'lx','ly'}, use_global_device_ids=true, to_apply=%region_24.27 | all-reduce | flops 16 | bytes 128 | tf_op jit(solution)/shard_map/psum | solution.py:53
  (147 shorter events, 86.7 us)
Async XLA Ops:
  6.5 172.1 %all-reduce.8.cloned.1.call-start = ((), (), s32[]{:S(2)}) async-start(), calls=%async_computation | async-start | bytes 1048576 | tf_op jit(solution)/shard_map/psum | solution.py:22
  7.4 4.5 collective-permute-start
  10.5 8.1 copy-start.6
  10.5 15.1 copy-start
  10.5 4.9 collective-permute-start.1
  16.5 2.1 copy-start.7
  16.5 5.2 collective-permute-start.2
  16.7 9.0 collective-permute-start.3
  26.1 3.7 collective-permute-start.4
  26.2 4.9 collective-permute-start.5
  31.3 6.0 collective-permute-start.6
  34.6 5.1 collective-permute-start.7
  118.0 275.1 %all-reduce.10.cloned.1.call-start = ((), (), s32[]{:S(2)}) async-start(), calls=%async_computation.1 | async-start | bytes 1048576 | tf_op jit(solution)/shard_map/psum | solution.py:22
  178.6 75.1 %copy-start.5 = (f32[4,32768]{1,0:T(4,128)S(1)}, f32[4,32768]{1,0:T(4,128)}, u32[]{:S(2)}) copy-start(f32[4,32768]{1,0:T(4,128)} %all-reduce.8.cloned.1.call-done) | copy-start | bytes 1572868
  335.0 272.6 %all-reduce.12.cloned.1.call-start = ((), (), s32[]{:S(2)}) async-start(), calls=%async_computation.2 | async-start | bytes 1048576 | tf_op jit(solution)/shard_map/psum | solution.py:22
  393.1 75.1 %copy-start.2 = (f32[4,32768]{1,0:T(4,128)S(1)}, f32[4,32768]{1,0:T(4,128)}, u32[]{:S(2)}) copy-start(f32[4,32768]{1,0:T(4,128)} %all-reduce.10.cloned.1.call-done) | copy-start | bytes 1572868
  549.5 272.6 %all-reduce.14.cloned.1.call-start = ((), (), s32[]{:S(2)}) async-start(), calls=%async_computation.3 | async-start | bytes 1048576 | tf_op jit(solution)/shard_map/psum | solution.py:22
  607.6 75.1 %copy-start.3 = (f32[4,32768]{1,0:T(4,128)S(1)}, f32[4,32768]{1,0:T(4,128)}, u32[]{:S(2)}) copy-start(f32[4,32768]{1,0:T(4,128)} %all-reduce.12.cloned.1.call-done) | copy-start | bytes 1572868
  764.0 272.6 %all-reduce.16.cloned.1.call-start = ((), (), s32[]{:S(2)}) async-start(), calls=%async_computation.4 | async-start | bytes 1048576 | tf_op jit(solution)/shard_map/psum | solution.py:22
  822.1 75.1 %copy-start.4 = (f32[4,32768]{1,0:T(4,128)S(1)}, f32[4,32768]{1,0:T(4,128)}, u32[]{:S(2)}) copy-start(f32[4,32768]{1,0:T(4,128)} %all-reduce.14.cloned.1.call-done) | copy-start | bytes 1572868
  978.5 273.7 %all-reduce.18.cloned.1.call-start = ((), (), s32[]{:S(2)}) async-start(), calls=%async_computation.5 | async-start | bytes 1048576 | tf_op jit(solution)/shard_map/psum | solution.py:22
  1194.1 273.9 %all-reduce.20.cloned.1.call-start = ((), (), s32[]{:S(2)}) async-start(), calls=%async_computation.6 | async-start | bytes 1048576 | tf_op jit(solution)/shard_map/psum | solution.py:22
  1545.1 78.4 %copy-start.1 = (f32[4,32768]{1,0:T(4,128)S(1)}, f32[4,32768]{1,0:T(4,128)}, u32[]{:S(2)}) copy-start(f32[4,32768]{1,0:T(4,128)} %convolution_select_fusion.1) | copy-start | bytes 1572868
Sparse Core Ops, SparseCore 0:
  118.2 60.3 all-reduce.7
  335.1 57.9 all-reduce.9
  549.6 57.9 all-reduce.11
  764.1 57.9 all-reduce.13
  978.6 57.9 all-reduce.15
  1194.2 57.9 all-reduce.17
  1410.0 57.9 all-reduce.19
where the time goes:
time: 1640 us; the launch traced here: 1630 us
  blocking collectives  1090 us (66%)
  waiting for transfers between devices  427 us (26%)
  matrix products  69.2 us (4%)
  other arithmetic  19.4 us (1%)
    psum x8, blocking collectives, body(): lax.psum(jnp.dot(flat, flat.T, precision=highest), ('lx', 'ly')) / total  586 us
    psum x7, blocking collectives, body(): lax.psum(jnp.dot(shared, flat.T, precision=highest), ('lx', 'ly')) / total  501 us
    psum x7, waiting for transfers between devices, from_root(): return lax.psum(kept, axis)  408 us
  transfers between devices with their start and end apart: 15, of which 15 were waited for; matrix products, arithmetic and copies ran while one was open for 0% of the time, Pallas kernels for 0%

commit v1 on v0

--- a/solution.py
+++ b/solution.py
@@ -50,7 +50,13 @@
     mine = lax.axis_index("grp")
     result = jnp.zeros_like(flat)
     for h in range(lax.axis_size("grp")):
-        gram = lax.psum(jnp.dot(flat, flat.T, precision=highest), ("lx", "ly")) / total
+
+        def balance_the_cube(frame, shard_axis, comm_axis):
+            for b in (shard_axis, comm_axis):
+                frame = jax.lax.psum(frame, axis_name=b)
+            return frame
+
+        gram = balance_the_cube(jnp.dot(flat, flat.T, precision=highest), "lx", "ly") / total
         done = jnp.dot(lower_inverse(gram), flat, precision=highest)
         result = jnp.where(mine == h, done, result)
         shared = from_root(done, "grp", h)

time: 1640 us -> 1270 us (0.77)
  blocking collectives: 1090 us -> 706 us
    psum x8 -> x16, blocking collectives: 586 us -> 205 us  [balance_the_cube(): frame = jax.lax.psum(frame, axis_name=b)]
where the time goes in v1:
time: 1270 us; the launch traced here: 1260 us
  blocking collectives  706 us (56%)
  waiting for transfers between devices  437 us (34%)
  matrix products  69.2 us (5%)
  other arithmetic  19.4 us (2%)
  between operations  15.3 us (1%)
    psum x7, blocking collectives, body(): lax.psum(jnp.dot(shared, flat.T, precision=highest), ('lx', 'ly')) / total  501 us
    psum x7, waiting for transfers between devices, from_root(): return lax.psum(kept, axis)  419 us
    psum x16, blocking collectives, balance_the_cube(): frame = jax.lax.psum(frame, axis_name=b)  205 us
  transfers between devices with their start and end apart: 15, of which 15 were waited for; matrix products, arithmetic and copies ran while one was open for 0% of the time, Pallas kernels for 0%

profile of v1, /device:TPU:32, one launch (start us, length us, event | category | flops | bytes accessed | tf_op | source)
XLA Modules:
  0.0 1262.0 jit_solution(13069980462268563744)
XLA Ops:
  21.7 3.9 collective-permute-done.3
  42.6 8.4 psum.210
  51.0 15.4 %psum.211 = f32[4,4]{0,1:T(4,128)S(1)} all-reduce(f32[4,4]{0,1:T(4,128)S(1)} %psum.210), channel_id=1, replica_groups=mesh['grp'=8,'lx'=4,'ly'=8] {'ly'}, use_global_device_ids=true, to_apply=%region_2.3 | all-reduce | flops 16 | bytes 128 | tf_op jit(solution)/shard_map/psum | solution.py:56
  71.2 62.1 %all-reduce.8.cloned.1.call-done = f32[4,32768]{1,0:T(4,128)} async-done(((f32[4,32768]{1,0:T(4,128)}), f32[4,32768]{1,0:T(4,128)}) %all-reduce.8.cloned.1.call-update) | async-done | bytes 524304 | tf_op jit(solution)/shard_map/psum | solution.py:22
  136.9 71.6 %psum.213 = f32[4,4]{0,1:T(4,128)S(1)} all-reduce(f32[4,4]{0,1:T(4,128)S(1)} %fusion.99), channel_id=1, replica_groups=mesh['grp'=8,'lx'=4,'ly'=8] {'lx','ly'}, use_global_device_ids=true, to_apply=%region_6.9 | all-reduce | flops 16 | bytes 128 | tf_op jit(solution)/shard_map/psum | solution.py:63
  211.8 7.7 psum.214
  219.5 18.1 %psum.215 = f32[4,4]{0,1:T(4,128)S(1)} all-reduce(f32[4,4]{0,1:T(4,128)S(1)} %psum.214), channel_id=1, replica_groups=mesh['grp'=8,'lx'=4,'ly'=8] {'ly'}, use_global_device_ids=true, to_apply=%region_8.11 | all-reduce | flops 16 | bytes 128 | tf_op jit(solution)/shard_map/psum | solution.py:56
  242.0 59.5 %all-reduce.10.cloned.1.call-done = f32[4,32768]{1,0:T(4,128)} async-done(((f32[4,32768]{1,0:T(4,128)}), f32[4,32768]{1,0:T(4,128)}) %all-reduce.10.cloned.1.call-update) | async-done | bytes 524304 | tf_op jit(solution)/shard_map/psum | solution.py:22
  301.5 3.5 fusion.101
  305.0 71.6 %psum.217 = f32[4,4]{0,1:T(4,128)S(1)} all-reduce(f32[4,4]{0,1:T(4,128)S(1)} %fusion.101), channel_id=1, replica_groups=mesh['grp'=8,'lx'=4,'ly'=8] {'lx','ly'}, use_global_device_ids=true, to_apply=%region_10.13 | all-reduce | flops 16 | bytes 128 | tf_op jit(solution)/shard_map/psum | solution.py:63
  380.0 7.7 psum.218
  387.7 18.1 %psum.219 = f32[4,4]{0,1:T(4,128)S(1)} all-reduce(f32[4,4]{0,1:T(4,128)S(1)} %psum.218), channel_id=1, replica_groups=mesh['grp'=8,'lx'=4,'ly'=8] {'ly'}, use_global_device_ids=true, to_apply=%region_12.15 | all-reduce | flops 16 | bytes 128 | tf_op jit(solution)/shard_map/psum | solution.py:56
  410.4 59.3 %all-reduce.12.cloned.1.call-done = f32[4,32768]{1,0:T(4,128)} async-done(((f32[4,32768]{1,0:T(4,128)}), f32[4,32768]{1,0:T(4,128)}) %all-reduce.12.cloned.1.call-update) | async-done | bytes 524304 | tf_op jit(solution)/shard_map/psum | solution.py:22
  473.2 71.6 %psum.221 = f32[4,4]{0,1:T(4,128)S(1)} all-reduce(f32[4,4]{0,1:T(4,128)S(1)} %fusion.103), channel_id=1, replica_groups=mesh['grp'=8,'lx'=4,'ly'=8] {'lx','ly'}, use_global_device_ids=true, to_apply=%region_14.17 | all-reduce | flops 16 | bytes 128 | tf_op jit(solution)/shard_map/psum | solution.py:63
  548.2 7.7 psum.222
  555.9 18.1 %psum.223 = f32[4,4]{0,1:T(4,128)S(1)} all-reduce(f32[4,4]{0,1:T(4,128)S(1)} %psum.222), channel_id=1, replica_groups=mesh['grp'=8,'lx'=4,'ly'=8] {'ly'}, use_global_device_ids=true, to_apply=%region_16.19 | all-reduce | flops 16 | bytes 128 | tf_op jit(solution)/shard_map/psum | solution.py:56
  578.4 59.5 %all-reduce.14.cloned.1.call-done = f32[4,32768]{1,0:T(4,128)} async-done(((f32[4,32768]{1,0:T(4,128)}), f32[4,32768]{1,0:T(4,128)}) %all-reduce.14.cloned.1.call-update) | async-done | bytes 524304 | tf_op jit(solution)/shard_map/psum | solution.py:22
  641.4 71.6 %psum.225 = f32[4,4]{0,1:T(4,128)S(1)} all-reduce(f32[4,4]{0,1:T(4,128)S(1)} %fusion.105), channel_id=1, replica_groups=mesh['grp'=8,'lx'=4,'ly'=8] {'lx','ly'}, use_global_device_ids=true, to_apply=%region_18.21 | all-reduce | flops 16 | bytes 128 | tf_op jit(solution)/shard_map/psum | solution.py:63
  716.3 7.7 psum.226
  724.1 18.1 %psum.227 = f32[4,4]{0,1:T(4,128)S(1)} all-reduce(f32[4,4]{0,1:T(4,128)S(1)} %psum.226), channel_id=1, replica_groups=mesh['grp'=8,'lx'=4,'ly'=8] {'ly'}, use_global_device_ids=true, to_apply=%region_20.23 | all-reduce | flops 16 | bytes 128 | tf_op jit(solution)/shard_map/psum | solution.py:56
  747.0 59.1 %all-reduce.16.cloned.1.call-done = f32[4,32768]{1,0:T(4,128)} async-done(((f32[4,32768]{1,0:T(4,128)}), f32[4,32768]{1,0:T(4,128)}) %all-reduce.16.cloned.1.call-update) | async-done | bytes 524304 | tf_op jit(solution)/shard_map/psum | solution.py:22
  809.5 71.6 %psum.229 = f32[4,4]{0,1:T(4,128)S(1)} all-reduce(f32[4,4]{0,1:T(4,128)S(1)} %fusion.107), channel_id=1, replica_groups=mesh['grp'=8,'lx'=4,'ly'=8] {'lx','ly'}, use_global_device_ids=true, to_apply=%region_22.25 | all-reduce | flops 16 | bytes 128 | tf_op jit(solution)/shard_map/psum | solution.py:63
  885.5 7.7 psum.230
  893.2 18.1 %psum.231 = f32[4,4]{0,1:T(4,128)S(1)} all-reduce(f32[4,4]{0,1:T(4,128)S(1)} %psum.230), channel_id=1, replica_groups=mesh['grp'=8,'lx'=4,'ly'=8] {'ly'}, use_global_device_ids=true, to_apply=%region_24.27 | all-reduce | flops 16 | bytes 128 | tf_op jit(solution)/shard_map/psum | solution.py:56
  915.9 59.5 %all-reduce.18.cloned.1.call-done = f32[4,32768]{1,0:T(4,128)} async-done(((f32[4,32768]{1,0:T(4,128)}), f32[4,32768]{1,0:T(4,128)}) %all-reduce.18.cloned.1.call-update) | async-done | bytes 524304 | tf_op jit(solution)/shard_map/psum | solution.py:22
  978.8 71.6 %psum.233 = f32[4,4]{0,1:T(4,128)S(1)} all-reduce(f32[4,4]{0,1:T(4,128)S(1)} %fusion.109), channel_id=1, replica_groups=mesh['grp'=8,'lx'=4,'ly'=8] {'lx','ly'}, use_global_device_ids=true, to_apply=%region_26.29 | all-reduce | flops 16 | bytes 128 | tf_op jit(solution)/shard_map/psum | solution.py:63
  1054.8 7.7 psum.234
  1062.5 18.3 %psum.235 = f32[4,4]{0,1:T(4,128)S(1)} all-reduce(f32[4,4]{0,1:T(4,128)S(1)} %psum.234), channel_id=1, replica_groups=mesh['grp'=8,'lx'=4,'ly'=8] {'ly'}, use_global_device_ids=true, to_apply=%region_28.31 | all-reduce | flops 16 | bytes 128 | tf_op jit(solution)/shard_map/psum | solution.py:56
  1085.3 59.6 %all-reduce.20.cloned.1.call-done = f32[4,32768]{1,0:T(4,128)} async-done(((f32[4,32768]{1,0:T(4,128)}), f32[4,32768]{1,0:T(4,128)}) %all-reduce.20.cloned.1.call-update) | async-done | bytes 524304 | tf_op jit(solution)/shard_map/psum | solution.py:22
  1148.4 71.6 %psum.237 = f32[4,4]{0,1:T(4,128)S(1)} all-reduce(f32[4,4]{0,1:T(4,128)S(1)} %fusion.111), channel_id=1, replica_groups=mesh['grp'=8,'lx'=4,'ly'=8] {'lx','ly'}, use_global_device_ids=true, to_apply=%region_30.33 | all-reduce | flops 16 | bytes 128 | tf_op jit(solution)/shard_map/psum | solution.py:63
  1224.4 7.7 psum.238
  1232.1 18.1 %psum.239 = f32[4,4]{0,1:T(4,128)S(1)} all-reduce(f32[4,4]{0,1:T(4,128)S(1)} %psum.238), channel_id=1, replica_groups=mesh['grp'=8,'lx'=4,'ly'=8] {'ly'}, use_global_device_ids=true, to_apply=%region_32.35 | all-reduce | flops 16 | bytes 128 | tf_op jit(solution)/shard_map/psum | solution.py:56
  (155 shorter events, 114.5 us)
Async XLA Ops:
  6.5 126.8 %all-reduce.8.cloned.1.call-start = ((), (), s32[]{:S(2)}) async-start(), calls=%async_computation | async-start | bytes 1048576 | tf_op jit(solution)/shard_map/psum | solution.py:22
  7.4 4.5 collective-permute-start
  10.5 8.1 copy-start.6
  10.5 15.1 %copy-start = (f32[4,64,512]{2,1,0:T(8,128)S(1)}, f32[4,64,512]{2,1,0:T(8,128)}, u32[]{:S(2)}) copy-start(f32[4,64,512]{2,1,0:T(8,128)} %param.8) | copy-start | bytes 1572868
  10.5 4.9 collective-permute-start.1
  16.5 2.1 copy-start.7
  16.5 5.2 collective-permute-start.2
  16.7 9.0 collective-permute-start.3
  26.1 3.7 collective-permute-start.4
  26.2 4.9 collective-permute-start.5
  31.3 6.0 collective-permute-start.6
  34.6 5.1 collective-permute-start.7
  71.0 230.6 %all-reduce.10.cloned.1.call-start = ((), (), s32[]{:S(2)}) async-start(), calls=%async_computation.1 | async-start | bytes 1048576 | tf_op jit(solution)/shard_map/psum | solution.py:22
  133.3 75.1 %copy-start.5 = (f32[4,32768]{1,0:T(4,128)S(1)}, f32[4,32768]{1,0:T(4,128)}, u32[]{:S(2)}) copy-start(f32[4,32768]{1,0:T(4,128)} %all-reduce.8.cloned.1.call-done) | copy-start | bytes 1572868
  242.0 227.7 %all-reduce.12.cloned.1.call-start = ((), (), s32[]{:S(2)}) async-start(), calls=%async_computation.2 | async-start | bytes 1048576 | tf_op jit(solution)/shard_map/psum | solution.py:22
  301.5 75.1 %copy-start.2 = (f32[4,32768]{1,0:T(4,128)S(1)}, f32[4,32768]{1,0:T(4,128)}, u32[]{:S(2)}) copy-start(f32[4,32768]{1,0:T(4,128)} %all-reduce.10.cloned.1.call-done) | copy-start | bytes 1572868
  410.1 227.7 %all-reduce.14.cloned.1.call-start = ((), (), s32[]{:S(2)}) async-start(), calls=%async_computation.3 | async-start | bytes 1048576 | tf_op jit(solution)/shard_map/psum | solution.py:22
  469.7 75.1 %copy-start.3 = (f32[4,32768]{1,0:T(4,128)S(1)}, f32[4,32768]{1,0:T(4,128)}, u32[]{:S(2)}) copy-start(f32[4,32768]{1,0:T(4,128)} %all-reduce.12.cloned.1.call-done) | copy-start | bytes 1572868
  578.3 227.7 %all-reduce.16.cloned.1.call-start = ((), (), s32[]{:S(2)}) async-start(), calls=%async_computation.4 | async-start | bytes 1048576 | tf_op jit(solution)/shard_map/psum | solution.py:22
  637.9 75.1 %copy-start.4 = (f32[4,32768]{1,0:T(4,128)S(1)}, f32[4,32768]{1,0:T(4,128)}, u32[]{:S(2)}) copy-start(f32[4,32768]{1,0:T(4,128)} %all-reduce.14.cloned.1.call-done) | copy-start | bytes 1572868
  746.5 228.9 %all-reduce.18.cloned.1.call-start = ((), (), s32[]{:S(2)}) async-start(), calls=%async_computation.5 | async-start | bytes 1048576 | tf_op jit(solution)/shard_map/psum | solution.py:22
  915.8 229.1 %all-reduce.20.cloned.1.call-start = ((), (), s32[]{:S(2)}) async-start(), calls=%async_computation.6 | async-start | bytes 1048576 | tf_op jit(solution)/shard_map/psum | solution.py:22
  1222.0 30.6 %copy-start.1 = (f32[4,32768]{1,0:T(4,128)S(1)}, f32[4,32768]{1,0:T(4,128)}, u32[]{:S(2)}) copy-start(f32[4,32768]{1,0:T(4,128)} %convolution_select_fusion.1) | copy-start | bytes 1572868
Sparse Core Ops, SparseCore 0:
  71.1 62.2 all-reduce.7
  242.1 59.3 all-reduce.9
  410.3 59.3 all-reduce.11
  578.4 59.3 all-reduce.13
  746.6 59.3 all-reduce.15
  915.9 59.3 all-reduce.17
  1085.4 59.4 all-reduce.19
